TPU v7x, 32 devices: a whole 2x2x4 slice. The times are simulated.
32 devices in a mesh: inst: 2 (over y), space: 16 (over z, x, core).
Axes of the slice: x: 2, y: 2, z: 4, core: 2. Of those that a mesh axis runs over, the one named last changes fastest.
Arguments:
- flow_state: float32 [4, 4, 192, 8, 512], P('inst', None, 'space'), may hold values from -6 to 6
- radial_first: float32 [512, 512], replicated, may hold values from -0.25 to 0.25
- radial_second: float32 [512, 512], replicated, may hold values from -0.25 to 0.25
- radial_flow: float32 [192, 512], P('space'), may hold values from -6 to 6
- swirl_flow: float32 [512, 192], replicated, may hold values from -6 to 6
- radius_inverse: float32 [512], replicated, may hold values from 0.05 to 1
- radial_flux: float32 [4, 4], replicated, may hold values from -3 to 3
- swirl_flux: float32 [4, 4], replicated, may hold values from -3 to 3
- cross_flux: float32 [4, 4], replicated, may hold values from -3 to 3
- span_flux: float32 [4, 4], replicated, may hold values from -3 to 3
- frequency: float32 [1], replicated, may hold values from 0.5 to 1.5
- viscosity: float32 [1], replicated, may hold values from 0.05 to 0.3
Outputs:
- residual: float32 [4, 4, 192, 8, 512], P('inst', None, 'space')
All inputs are finite; a program needn't handle non-finite values.
Results may differ from a plain program's by a relative error of at most 0.000055.
Values sent between devices are 32-bit elements; how exact they have to be, the bound alone decides.
A program may use at most 64 MiB of HBM per device.

v0:
```python
import functools
import math

import jax
import jax.numpy as jnp
import numpy as np
from jax import lax
from jax.experimental import pallas as pl
from jax.experimental.pallas import tpu as pltpu
from jax.sharding import PartitionSpec as P

highest = lax.Precision.HIGHEST


def spectral(points):
    indices = jnp.arange(points)
    offsets = (indices[:, None] - indices[None, :]) % points
    spacing = 2.0 * math.pi / points
    angles = offsets.astype(jnp.float32) * (math.pi / points)
    parity = (1 - 2 * (offsets % 2)).astype(jnp.float32)
    nonzero = offsets != 0
    sines = jnp.where(nonzero, jnp.sin(angles), jnp.float32(1.0))
    first = jnp.where(nonzero, 0.5 * parity * jnp.cos(angles) / sines, jnp.float32(0.0))
    diagonal_value = -math.pi**2 / (3.0 * spacing**2) - 1.0 / 6.0
    second = jnp.where(nonzero, -0.5 * parity / (sines * sines), jnp.float32(diagonal_value))
    return (first, second)


def apply_flux(matrix, fields):
    return jnp.einsum("uv,iv...->iu...", matrix, fields, precision=highest)


def on_device_lines(
    flow_state,
    radial_first,
    radial_second,
    radial_flow,
    swirl_flow,
    radius_inverse,
    radial_flux,
    swirl_flux,
    cross_flux,
    span_flux,
    frequency,
    viscosity,
):
    inst_dev = flow_state.shape[0]
    n_inst = lax.axis_size("inst")
    n_space = lax.axis_size("space")
    instances = inst_dev * n_inst
    time_matrix, unused = spectral(instances)
    azimuth = swirl_flow.shape[1]
    radial = flow_state.shape[4]
    planes = flow_state.shape[3]
    turn_first, turn_second = spectral(azimuth)
    spacing = 2.0 * math.pi / azimuth
    turn_first = spacing * turn_first
    turn_second = spacing * spacing * turn_second
    viscous = viscosity[0]
    radial_slope = jnp.einsum("ivtzs,rs->ivtzr", flow_state, radial_first, precision=highest)
    radial_curve = jnp.einsum("ivtzs,rs->ivtzr", flow_state, radial_second, precision=highest)
    lane = math.gcd(radial, planes * radial // n_space)
    row_total = planes * radial // lane
    shape_rows = flow_state.shape[:3] + (row_total, lane)
    state_rows = flow_state.reshape(shape_rows)
    slope_rows = radial_slope.reshape(shape_rows)
    fields = lax.all_to_all(state_rows, "space", split_axis=3, concat_axis=2, tiled=True)
    slopes = lax.all_to_all(slope_rows, "space", split_axis=3, concat_axis=2, tiled=True)
    row_offset = lax.axis_index("space") * fields.shape[3]
    turning_fields = fields
    turning_slopes = slopes
    item_count = turning_fields.shape[0]
    variables = turning_fields.shape[1]
    count = turning_fields.shape[3]
    lane = turning_fields.shape[4]
    width = count * lane
    row_ids = row_offset + jnp.arange(count, dtype=jnp.int32)
    blocks = row_ids % (radial // lane)
    point_ids = (blocks[:, None] * lane + jnp.arange(lane, dtype=jnp.int32)[None, :]).reshape(width)
    inverse_tile = jnp.take(radius_inverse, point_ids)
    swirl_tile = jnp.take(swirl_flow, point_ids, axis=0).T * inverse_tile[None, :]
    turning_fields = turning_fields.reshape(item_count, variables, azimuth, width)
    turning_slopes = turning_slopes.reshape(item_count, variables, azimuth, width)
    turn_slope = jnp.einsum("st,ivtc->ivsc", turn_first, turning_fields, precision=highest)
    turn_curve = jnp.einsum("st,ivtc->ivsc", turn_second, turning_fields, precision=highest)
    cross_slope = jnp.einsum("st,ivtc->ivsc", turn_first, turning_slopes, precision=highest)
    turned_term = swirl_tile * turn_slope + inverse_tile * apply_flux(swirl_flux, turn_slope)
    turned_term = turned_term + inverse_tile * apply_flux(cross_flux, cross_slope)
    turned_term = turned_term - viscous * (inverse_tile * inverse_tile) * turn_curve
    result = lax.all_to_all(
        turned_term.reshape(item_count, variables, azimuth, count, lane),
        "space",
        split_axis=2,
        concat_axis=3,
        tiled=True,
    )
    turned = result.reshape(flow_state.shape)
    own_rows = lax.dynamic_slice_in_dim(time_matrix, lax.axis_index("inst") * inst_dev, inst_dev, 0)
    mixed_out = jnp.einsum(
        "nm,mvtzr->nvtzr",
        own_rows,
        lax.all_gather(flow_state, "inst", axis=0, tiled=True),
        precision=highest,
    )
    far_terms = frequency[0] * mixed_out + turned
    upper = jnp.roll(flow_state, -1, axis=3)
    lower = jnp.roll(flow_state, 1, axis=3)
    span_slope = 0.5 * (upper - lower)
    span_curve = upper + lower - 2.0 * flow_state
    radial_part = radial_flow[:, None, :] * radial_slope + apply_flux(radial_flux, radial_slope)
    radial_part = radial_part - viscous * (radial_curve + radius_inverse * radial_slope)
    radial_part = radial_part + apply_flux(span_flux, span_slope) - viscous * span_curve
    return far_terms + radial_part


LANE = 128
SUBLANE = 8
NT = (((1,), (1,)), ((), ()))
NN = (((1,), (0,)), ((), ()))


def spectral_table(points):
    index = np.arange(points)
    k = (index[:, None] - index[None, :]) % points
    h = 2.0 * math.pi / points
    angle = math.pi * k / points
    sign = 1.0 - 2.0 * (k % 2)
    sine = np.where(k != 0, np.sin(angle), 1.0)
    first = np.where(k != 0, 0.5 * sign * np.cos(angle) / sine, 0.0)
    second = np.where(k != 0, -0.5 * sign / sine**2, -(math.pi**2) / (3.0 * h * h) - 1.0 / 6.0)
    return first.astype(np.float32), second.astype(np.float32)


def halves(x):
    high = x.astype(jnp.bfloat16)
    return high, (x - high.astype(jnp.float32)).astype(jnp.bfloat16)


def dot3(a, b, dims):
    dot = functools.partial(
        lax.dot_general, dimension_numbers=dims, preferred_element_type=jnp.float32
    )
    return dot(a[0], b[0]) + (dot(a[0], b[1]) + dot(a[1], b[0]))


def slab_kernel(
    n_space,
    n_inst,
    time_row,
    state,
    first,
    second,
    radial_flow,
    swirl_flow,
    inverse,
    turn_high,
    turn_low,
    radial_flux,
    swirl_flux,
    cross_flux,
    span_flux,
    frequency,
    viscosity,
    out,
    outgoing,
    fields,
    turned,
    returned,
    mates,
    local,
    mixed,
    base,
    slope,
    curve,
    swirl,
    first_high,
    first_low,
    second_high,
    second_low,
    send1,
    recv1,
    send2,
    recv2,
    own_sem,
    mate_send,
    mate_recv,
):
    inst_dev, variables, azimuth_dev, planes, radial = state.shape
    azimuth = azimuth_dev * n_space
    blocks = radial // LANE
    per = SUBLANE // blocks
    chunks = variables // per
    span = azimuth_dev * SUBLANE
    me = lax.axis_index("space")
    inst_me = lax.axis_index("inst")
    order = sorted(range(1, n_space), key=lambda k: abs(2 * k - n_space))

    barrier = pltpu.get_barrier_semaphore()
    for k in order:
        pl.semaphore_signal(barrier, inc=1, device_id={"space": lax.rem(me + k, n_space)})
    for k in range(1, n_inst):
        pl.semaphore_signal(barrier, inc=1, device_id={"inst": lax.rem(inst_me + k, n_inst)})

    def at(index):
        return pl.ds(pl.multiple_of(index * span, SUBLANE), span)

    def exchange(source, target, send, recv, c, k):
        peer = lax.rem(me + k, n_space)
        return pltpu.make_async_remote_copy(
            src_ref=source.at[c, at(peer)],
            dst_ref=target.at[c, at(me)],
            send_sem=send.at[c, k],
            recv_sem=recv.at[c, k],
            device_id={"space": peer},
        )

    def own(source, target, stage, c):
        return pltpu.make_async_copy(
            source.at[c, at(me)], target.at[c, at(me)], own_sem.at[stage, c]
        )

    def mate(k):
        return pltpu.make_async_remote_copy(
            src_ref=state,
            dst_ref=mates.at[k - 1],
            send_sem=mate_send.at[k - 1],
            recv_sem=mate_recv.at[k - 1],
            device_id={"inst": lax.rem(inst_me + k, n_inst)},
        )

    def send_all(source, target, send, recv, stage, c):
        for k in order:
            exchange(source, target, send, recv, c, k).start()
        own(source, target, stage, c).start()

    def await_all(source, target, send, recv, stage, c):
        for k in order:
            exchange(source, target, send, recv, c, k).wait_recv()
        own(source, target, stage, c).wait()

    def pack(c):
        for i in range(inst_dev):
            for w in range(per):
                for t in range(azimuth_dev):
                    for b in range(blocks):
                        row = i * planes * span + t * SUBLANE + w * blocks + b
                        outgoing[c, pl.ds(row, planes, stride=span), :] = state[
                            i, c * per + w, t, :, b * LANE : (b + 1) * LANE
                        ]

    for c in range(chunks):
        pack(c)
        if c == 0:
            pl.semaphore_wait(barrier, n_space - 1 + n_inst - 1)
        send_all(outgoing, fields, send1, recv1, 0, c)
    for k in range(1, n_inst):
        mate(k).start()

    q = inverse[...]
    viscous = viscosity[0]
    first_high[...], first_low[...] = halves(first[...])
    second_high[...], second_low[...] = halves(second[...])
    first_pair = (first_high, first_low)
    second_pair = (second_high, second_low)
    swirl[...] = swirl_flow[...].T * q
    turn_rate = -viscous * q * q

    def read(pair):
        return pair[0][...], pair[1][...]

    rows = azimuth_dev * planes

    @pl.loop(0, inst_dev)
    def _(i):
        for v in range(variables):
            own_state = halves(state[i, v].reshape(rows, radial))
            slope[v] = dot3(own_state, read(first_pair), NT).reshape(azimuth_dev, planes, radial)
            curve[v] = dot3(own_state, read(second_pair), NT).reshape(azimuth_dev, planes, radial)

        @pl.loop(0, azimuth_dev)
        def _(t):
            flow_rate = radial_flow[pl.ds(t, 1), :] - viscous * q
            values = [state[i, v, t] for v in range(variables)]
            uppers = [pltpu.roll(x, planes - 1, 0) for x in values]
            lowers = [pltpu.roll(x, 1, 0) for x in values]
            steps = [0.5 * (up - low) for up, low in zip(uppers, lowers)]
            slopes = [slope[v, t] for v in range(variables)]
            for u in range(variables):
                bend = uppers[u] + lowers[u] - 2.0 * values[u]
                total = flow_rate * slopes[u] - viscous * (curve[u, t] + bend)
                for v in range(variables):
                    total = total + radial_flux[u, v] * slopes[v] + span_flux[u, v] * steps[v]
                local[i, u, t] = total

    for c in range(chunks):
        await_all(outgoing, fields, send1, recv1, 0, c)
        for w in range(per):
            v = c * per + w
            field = jnp.concatenate(
                [
                    fields[c, pl.ds(w * blocks + b, azimuth, stride=SUBLANE), :]
                    for b in range(blocks)
                ],
                axis=1,
            )
            split = halves(field)
            field_slope = dot3(split, read(first_pair), NT)
            for u in range(variables):
                term = swirl_flux[u, v] * field + cross_flux[u, v] * field_slope
                mixed[u] = mixed[u] + term if v else term
            turn = dot3((turn_high[...], turn_low[...]), split, NN)
            base[v] = swirl[...] * turn[:azimuth] + turn_rate * turn[azimuth:]

    for c in range(chunks):
        for w in range(per):
            u = c * per + w
            turn = dot3((turn_high[:azimuth], turn_low[:azimuth]), halves(mixed[u]), NN)
            total = base[u] + q * turn
            for b in range(blocks):
                turned[c, pl.ds(w * blocks + b, azimuth, stride=SUBLANE), :] = total[
                    :, b * LANE : (b + 1) * LANE
                ]
        send_all(turned, returned, send2, recv2, 1, c)

    for k in range(1, n_inst):
        mate(k).wait()
    instances = inst_dev * n_inst

    @pl.loop(0, variables)
    def _(v):
        @pl.loop(0, azimuth_dev)
        def _(t):
            for n in range(inst_dev):
                total = local[n, v, t]
                for k in range(n_inst):
                    for m in range(inst_dev):
                        offset = (n - m + k * inst_dev) % instances
                        value = state[m, v, t] if k == 0 else mates[k - 1, m, v, t]
                        total = total + (frequency[0] * time_row[offset]) * value
                local[n, v, t] = total

    for c in range(chunks):
        await_all(turned, returned, send2, recv2, 1, c)
        for i in range(inst_dev):
            for w in range(per):
                for t in range(azimuth_dev):
                    for b in range(blocks):
                        row = i * planes * span + t * SUBLANE + w * blocks + b
                        lanes = slice(b * LANE, (b + 1) * LANE)
                        out[i, c * per + w, t, :, lanes] = (
                            local[i, c * per + w, t, :, lanes]
                            + returned[c, pl.ds(row, planes, stride=span), :]
                        )
    for c in range(chunks):
        for k in order:
            exchange(outgoing, fields, send1, recv1, c, k).wait_send()
            exchange(turned, returned, send2, recv2, c, k).wait_send()


def on_device(
    flow_state,
    radial_first,
    radial_second,
    radial_flow,
    swirl_flow,
    radius_inverse,
    radial_flux,
    swirl_flux,
    cross_flux,
    span_flux,
    frequency,
    viscosity,
):
    inst_dev, variables, azimuth_dev, planes, radial = flow_state.shape
    n_inst = lax.axis_size("inst")
    n_space = lax.axis_size("space")
    azimuth = swirl_flow.shape[1]
    blocks = radial // LANE
    chunks = variables * blocks // SUBLANE
    time_row = [float(x) for x in spectral_table(inst_dev * n_inst)[0][:, 0]]
    turn_first, turn_second = spectral_table(azimuth)
    h = np.float32(2.0 * math.pi / azimuth)
    turn = np.concatenate([h * turn_first, h * h * turn_second])
    turn_high = turn.astype(jnp.bfloat16)
    turn_low = (turn - turn_high.astype(np.float32)).astype(jnp.bfloat16)
    vmem = pl.BlockSpec(memory_space=pltpu.VMEM)
    smem = pl.BlockSpec(memory_space=pltpu.SMEM)
    packed = pltpu.VMEM((chunks, n_space * azimuth_dev * SUBLANE, LANE), jnp.float32)
    slab = pltpu.VMEM((variables, azimuth, radial), jnp.float32)
    pencil = pltpu.VMEM((variables, azimuth_dev, planes, radial), jnp.float32)
    square = pltpu.VMEM((radial, radial), jnp.bfloat16)
    sems = pltpu.SemaphoreType.DMA((chunks, n_space))
    return pl.pallas_call(
        functools.partial(slab_kernel, n_space, n_inst, time_row),
        out_shape=jax.ShapeDtypeStruct(flow_state.shape, jnp.float32),
        in_specs=[vmem] * 8 + [smem] * 6,
        out_specs=vmem,
        scratch_shapes=[
            packed,
            packed,
            packed,
            packed,
            pltpu.VMEM((n_inst - 1,) + flow_state.shape, jnp.float32),
            pltpu.VMEM(flow_state.shape, jnp.float32),
            slab,
            slab,
            pencil,
            pencil,
            pltpu.VMEM((azimuth, radial), jnp.float32),
            square,
            square,
            square,
            square,
            sems,
            sems,
            sems,
            sems,
            pltpu.SemaphoreType.DMA((2, chunks)),
            pltpu.SemaphoreType.DMA((n_inst - 1,)),
            pltpu.SemaphoreType.DMA((n_inst - 1,)),
        ],
        compiler_params=pltpu.CompilerParams(
            collective_id=0, has_side_effects=True, vmem_limit_bytes=56 * 1024 * 1024
        ),
    )(
        flow_state,
        radial_first,
        radial_second,
        radial_flow,
        swirl_flow,
        radius_inverse.reshape(1, radial),
        jnp.asarray(turn_high),
        jnp.asarray(turn_low),
        radial_flux,
        swirl_flux,
        cross_flux,
        span_flux,
        frequency,
        viscosity,
    )


def residual_on_device(flow_state, *rest):
    inst_dev, variables, azimuth_dev, planes, radial = flow_state.shape
    blocks = radial // LANE
    slabs = (
        inst_dev * planes == lax.axis_size("space")
        and lax.axis_size("inst") > 1
        and planes == SUBLANE
        and radial == blocks * LANE
        and SUBLANE % blocks == 0
        and variables * blocks % SUBLANE == 0
    )
    return (on_device if slabs else on_device_lines)(flow_state, *rest)


def solution(mesh):
    in_specs = (
        P("inst", None, "space", None, None),
        P(),
        P(),
        P("space", None),
        P(),
        P(),
        P(),
        P(),
        P(),
        P(),
        P(),
        P(),
    )
    out_specs = P("inst", None, "space", None, None)
    return jax.shard_map(
        residual_on_device, mesh=mesh, in_specs=in_specs, out_specs=out_specs, check_vma=False
    )
```

profile of v0, /device:TPU:0, one launch (start us, length us, event | category | flops | bytes accessed | tf_op | source)
XLA Modules:
  0.0 85.9 jit_solution(6951281369317550935)
XLA Ops:
  1.3 2.0 %copy.15.swirl_flow = f32[512,192]{1,0:T(8,128)} copy(f32[512,192]{0,1:T(8,128)} %param.18) | data formatting | bytes 786432 | tf_op args[4]
  3.3 80.0 %shard_map.136 = f32[2,4,12,8,512]{4,3,2,1,0:T(8,128)} custom-call(f32[2,4,12,8,512]{4,3,2,1,0:T(8,128)} %state.1, f32[512,512]{1,0:T(8,128)} %first.1, f32[512,512]{1,0:T(8,128)} %second.1, f32[12,512]{1,0:T(8,128)} %radial_flow.1, f32[512,192]{1,0:T(8,128)} %copy.15.swirl_flow, f32[1,512]{1,0:T(1,128)} %bitcast.1, ...), custom_call_target="tpu_custom_call" | custom-call | tf_op jit(solution)/shard_map/pallas_call | solution.py:393
  83.3 2.7 %copy.19 = f32[2,4,12,8,512]{4,3,2,1,0:T(8,128)} copy(f32[2,4,12,8,512]{4,3,2,1,0:T(8,128)} %shard_map.136) | data formatting | bytes 3145728
where the time goes:
time: 86.1 us; the launch traced here: 85.9 us
  Pallas kernels  80 us (93%)
  local copies, waits for them, and re-layouts  4.66 us (5%)
  between operations  1.31 us (2%)
    pallas_call x1, Pallas kernels, on_device(): pl.pallas_call(functools.partial(slab_kernel, n_space, n_inst, time_row),...  80 us
    unnamed x2, local copies, waits for them, and re-layouts  4.66 us

commit v1 on v0

--- a/solution.py
+++ b/solution.py
@@ -147,11 +147,11 @@
     n_space,
     n_inst,
     time_row,
-    state,
-    first,
-    second,
+    state_in,
+    first_in,
+    second_in,
+    swirl_in,
     radial_flow,
-    swirl_flow,
     inverse,
     turn_high,
     turn_low,
@@ -162,6 +162,9 @@
     frequency,
     viscosity,
     out,
+    state,
+    first,
+    second,
     outgoing,
     fields,
     turned,
@@ -177,6 +180,8 @@
     first_low,
     second_high,
     second_low,
+    last_high,
+    last_low,
     send1,
     recv1,
     send2,
@@ -184,19 +189,39 @@
     own_sem,
     mate_send,
     mate_recv,
+    load_sem,
 ):
     inst_dev, variables, azimuth_dev, planes, radial = state.shape
     azimuth = azimuth_dev * n_space
     blocks = radial // LANE
-    per = SUBLANE // blocks
-    chunks = variables // per
-    span = azimuth_dev * SUBLANE
+    chunks = variables
+    span = azimuth_dev * blocks
     me = lax.axis_index("space")
     inst_me = lax.axis_index("inst")
-    order = sorted(range(1, n_space), key=lambda k: abs(2 * k - n_space))
+    half = n_space // 2
+    quarter = max(n_space // 4, 1)
+    upper_half = me // half
+    depth = upper_half * (n_space - 1 - me) + (1 - upper_half) * me
+    shift = (depth // quarter) % 2 * (quarter - 1)
+    heading = 1 - 2 * upper_half
+    others = range(1, n_space)
+
+    def load_state(c):
+        return pltpu.make_async_copy(state_in.at[:, c], state.at[:, c], load_sem.at[c])
+
+    loads = [
+        pltpu.make_async_copy(source, target, load_sem.at[variables + n])
+        for n, (source, target) in enumerate(
+            [(first_in, first), (second_in, second), (swirl_in, swirl)]
+        )
+    ]
+    for c in range(chunks):
+        load_state(c).start()
+    for load in loads:
+        load.start()
 
     barrier = pltpu.get_barrier_semaphore()
-    for k in order:
+    for k in others:
         pl.semaphore_signal(barrier, inc=1, device_id={"space": lax.rem(me + k, n_space)})
     for k in range(1, n_inst):
         pl.semaphore_signal(barrier, inc=1, device_id={"inst": lax.rem(inst_me + k, n_inst)})
@@ -205,12 +230,13 @@
         return pl.ds(pl.multiple_of(index * span, SUBLANE), span)
 
     def exchange(source, target, send, recv, c, k):
-        peer = lax.rem(me + k, n_space)
+        step = 1 + lax.rem(k - 1 + shift, n_space - 1)
+        peer = lax.rem(me + heading * step + n_space, n_space)
         return pltpu.make_async_remote_copy(
             src_ref=source.at[c, at(peer)],
             dst_ref=target.at[c, at(me)],
             send_sem=send.at[c, k],
-            recv_sem=recv.at[c, k],
+            recv_sem=recv.at[c, me],
             device_id={"space": peer},
         )
 
@@ -229,26 +255,33 @@
         )
 
     def send_all(source, target, send, recv, stage, c):
-        for k in order:
+        for k in others:
             exchange(source, target, send, recv, c, k).start()
         own(source, target, stage, c).start()
 
     def await_all(source, target, send, recv, stage, c):
-        for k in order:
-            exchange(source, target, send, recv, c, k).wait_recv()
+        for k in others:
+            peer = lax.rem(me + k, n_space)
+            pltpu.make_async_remote_copy(
+                src_ref=source.at[c, at(peer)],
+                dst_ref=target.at[c, at(peer)],
+                send_sem=send.at[c, k],
+                recv_sem=recv.at[c, peer],
+                device_id={"space": peer},
+            ).wait_recv()
         own(source, target, stage, c).wait()
 
     def pack(c):
         for i in range(inst_dev):
-            for w in range(per):
-                for t in range(azimuth_dev):
-                    for b in range(blocks):
-                        row = i * planes * span + t * SUBLANE + w * blocks + b
-                        outgoing[c, pl.ds(row, planes, stride=span), :] = state[
-                            i, c * per + w, t, :, b * LANE : (b + 1) * LANE
-                        ]
+            for at_row in range(azimuth_dev * blocks):
+                step, block = divmod(at_row, blocks)
+                row = i * planes * span + at_row
+                outgoing[c, pl.ds(row, planes, stride=span), :] = state[
+                    i, c, step, :, block * LANE : (block + 1) * LANE
+                ]
 
     for c in range(chunks):
+        load_state(c).wait()
         pack(c)
         if c == 0:
             pl.semaphore_wait(barrier, n_space - 1 + n_inst - 1)
@@ -258,11 +291,13 @@
 
     q = inverse[...]
     viscous = viscosity[0]
+    for load in loads:
+        load.wait()
     first_high[...], first_low[...] = halves(first[...])
     second_high[...], second_low[...] = halves(second[...])
     first_pair = (first_high, first_low)
     second_pair = (second_high, second_low)
-    swirl[...] = swirl_flow[...].T * q
+    swirl[...] = swirl[...] * q
     turn_rate = -viscous * q * q
 
     def read(pair):
@@ -292,35 +327,33 @@
                     total = total + radial_flux[u, v] * slopes[v] + span_flux[u, v] * steps[v]
                 local[i, u, t] = total
 
-    for c in range(chunks):
-        await_all(outgoing, fields, send1, recv1, 0, c)
-        for w in range(per):
-            v = c * per + w
-            field = jnp.concatenate(
-                [
-                    fields[c, pl.ds(w * blocks + b, azimuth, stride=SUBLANE), :]
-                    for b in range(blocks)
-                ],
-                axis=1,
-            )
-            split = halves(field)
-            field_slope = dot3(split, read(first_pair), NT)
-            for u in range(variables):
-                term = swirl_flux[u, v] * field + cross_flux[u, v] * field_slope
-                mixed[u] = mixed[u] + term if v else term
-            turn = dot3((turn_high[...], turn_low[...]), split, NN)
-            base[v] = swirl[...] * turn[:azimuth] + turn_rate * turn[azimuth:]
-
-    for c in range(chunks):
-        for w in range(per):
-            u = c * per + w
-            turn = dot3((turn_high[:azimuth], turn_low[:azimuth]), halves(mixed[u]), NN)
-            total = base[u] + q * turn
-            for b in range(blocks):
-                turned[c, pl.ds(w * blocks + b, azimuth, stride=SUBLANE), :] = total[
-                    :, b * LANE : (b + 1) * LANE
-                ]
-        send_all(turned, returned, send2, recv2, 1, c)
+    def turn_base(v, split):
+        turn = dot3((turn_high[...], turn_low[...]), split, NN)
+        base[v] = swirl[...] * turn[:azimuth] + turn_rate * turn[azimuth:]
+
+    for v in range(variables):
+        await_all(outgoing, fields, send1, recv1, 0, v)
+        field = jnp.concatenate(
+            [fields[v, pl.ds(b, azimuth, stride=blocks), :] for b in range(blocks)], axis=1
+        )
+        split = halves(field)
+        field_slope = dot3(split, read(first_pair), NT)
+        if v < variables - 1:
+            turn_base(v, split)
+        else:
+            last_high[...], last_low[...] = split
+        for u in range(variables):
+            term = swirl_flux[u, v] * field + cross_flux[u, v] * field_slope
+            mixed[u] = mixed[u] + term if v else term
+
+    for u in range(variables):
+        if u == variables - 1:
+            turn_base(u, (last_high[...], last_low[...]))
+        turn = dot3((turn_high[:azimuth], turn_low[:azimuth]), halves(mixed[u]), NN)
+        total = base[u] + q * turn
+        for b in range(blocks):
+            turned[u, pl.ds(b, azimuth, stride=blocks), :] = total[:, b * LANE : (b + 1) * LANE]
+        send_all(turned, returned, send2, recv2, 1, u)
 
     for k in range(1, n_inst):
         mate(k).wait()
@@ -342,17 +375,16 @@
     for c in range(chunks):
         await_all(turned, returned, send2, recv2, 1, c)
         for i in range(inst_dev):
-            for w in range(per):
-                for t in range(azimuth_dev):
-                    for b in range(blocks):
-                        row = i * planes * span + t * SUBLANE + w * blocks + b
-                        lanes = slice(b * LANE, (b + 1) * LANE)
-                        out[i, c * per + w, t, :, lanes] = (
-                            local[i, c * per + w, t, :, lanes]
-                            + returned[c, pl.ds(row, planes, stride=span), :]
-                        )
+            for at_row in range(azimuth_dev * blocks):
+                step, block = divmod(at_row, blocks)
+                row = i * planes * span + at_row
+                lanes = slice(block * LANE, (block + 1) * LANE)
+                out[i, c, step, :, lanes] = (
+                    local[i, c, step, :, lanes]
+                    + returned[c, pl.ds(row, planes, stride=span), :]
+                )
     for c in range(chunks):
-        for k in order:
+        for k in others:
             exchange(outgoing, fields, send1, recv1, c, k).wait_send()
             exchange(turned, returned, send2, recv2, c, k).wait_send()
 
@@ -376,7 +408,6 @@
     n_space = lax.axis_size("space")
     azimuth = swirl_flow.shape[1]
     blocks = radial // LANE
-    chunks = variables * blocks // SUBLANE
     time_row = [float(x) for x in spectral_table(inst_dev * n_inst)[0][:, 0]]
     turn_first, turn_second = spectral_table(azimuth)
     h = np.float32(2.0 * math.pi / azimuth)
@@ -384,18 +415,23 @@
     turn_high = turn.astype(jnp.bfloat16)
     turn_low = (turn - turn_high.astype(np.float32)).astype(jnp.bfloat16)
     vmem = pl.BlockSpec(memory_space=pltpu.VMEM)
+    hbm = pl.BlockSpec(memory_space=pltpu.HBM)
     smem = pl.BlockSpec(memory_space=pltpu.SMEM)
-    packed = pltpu.VMEM((chunks, n_space * azimuth_dev * SUBLANE, LANE), jnp.float32)
+    packed = pltpu.VMEM((variables, azimuth * blocks, LANE), jnp.float32)
     slab = pltpu.VMEM((variables, azimuth, radial), jnp.float32)
     pencil = pltpu.VMEM((variables, azimuth_dev, planes, radial), jnp.float32)
+    half_slab = pltpu.VMEM((azimuth, radial), jnp.bfloat16)
     square = pltpu.VMEM((radial, radial), jnp.bfloat16)
-    sems = pltpu.SemaphoreType.DMA((chunks, n_space))
+    sems = pltpu.SemaphoreType.DMA((variables, n_space))
     return pl.pallas_call(
         functools.partial(slab_kernel, n_space, n_inst, time_row),
-        out_shape=jax.ShapeDtypeStruct(flow_state.shape, jnp.float32),
-        in_specs=[vmem] * 8 + [smem] * 6,
+        out_shape=pltpu.VMEM(flow_state.shape, jnp.float32),
+        in_specs=[hbm] * 4 + [vmem] * 4 + [smem] * 6,
         out_specs=vmem,
         scratch_shapes=[
+            pltpu.VMEM(flow_state.shape, jnp.float32),
+            pltpu.VMEM((radial, radial), jnp.float32),
+            pltpu.VMEM((radial, radial), jnp.float32),
             packed,
             packed,
             packed,
@@ -411,23 +447,26 @@
             square,
             square,
             square,
+            half_slab,
+            half_slab,
             sems,
             sems,
             sems,
             sems,
-            pltpu.SemaphoreType.DMA((2, chunks)),
+            pltpu.SemaphoreType.DMA((2, variables)),
             pltpu.SemaphoreType.DMA((n_inst - 1,)),
             pltpu.SemaphoreType.DMA((n_inst - 1,)),
+            pltpu.SemaphoreType.DMA((variables + 3,)),
         ],
         compiler_params=pltpu.CompilerParams(
-            collective_id=0, has_side_effects=True, vmem_limit_bytes=56 * 1024 * 1024
+            collective_id=0, has_side_effects=True, vmem_limit_bytes=59 * 1024 * 1024
         ),
     )(
         flow_state,
         radial_first,
         radial_second,
+        swirl_flow.T,
         radial_flow,
-        swirl_flow,
         radius_inverse.reshape(1, radial),
         jnp.asarray(turn_high),
         jnp.asarray(turn_low),
@@ -448,8 +487,7 @@
         and lax.axis_size("inst") > 1
         and planes == SUBLANE
         and radial == blocks * LANE
-        and SUBLANE % blocks == 0
-        and variables * blocks % SUBLANE == 0
+        and azimuth_dev * blocks % SUBLANE == 0
     )
     return (on_device if slabs else on_device_lines)(flow_state, *rest)
 

time: 86.1 us -> 83.9 us (0.974)
  local copies, waits for them, and re-layouts: 4.66 us -> 1.15 us
  Pallas kernels: 80 us -> 81.3 us
    unnamed x2 -> x1, local copies, waits for them, and re-layouts: 4.66 us -> 1.15 us
    pallas_call x1, Pallas kernels: 80 us -> 81.3 us  [on_device(): pl.pallas_call(functools.partial(slab_kernel, n_space, n_inst, time_row),...]
where the time goes in v1:
time: 83.9 us; the launch traced here: 83.8 us
  Pallas kernels  81.3 us (97%)
  between operations  1.3 us (2%)
  local copies, waits for them, and re-layouts  1.15 us (1%)
    pallas_call x1, Pallas kernels, on_device(): pl.pallas_call(functools.partial(slab_kernel, n_space, n_inst, time_row),...  81.3 us

profile of v1, /device:TPU:0, one launch (start us, length us, event | category | flops | bytes accessed | tf_op | source)
XLA Modules:
  0.0 83.8 jit_solution(16869182041530035113)
XLA Ops:
  1.3 81.3 %shard_map.136 = f32[2,4,12,8,512]{4,3,2,1,0:T(8,128)S(1)} custom-call(f32[2,4,12,8,512]{4,3,2,1,0:T(8,128)} %state_in.1, f32[512,512]{1,0:T(8,128)} %first_in.1, f32[512,512]{1,0:T(8,128)} %second_in.1, f32[192,512]{1,0:T(8,128)} %bitcast.2, f32[12,512]{1,0:T(8,128)} %radial_flow.1, f32[1,512]{1,0:T(1,128)} %bitcast.3, ...), custom_call_target="tpu_custom_call" | custom-call | tf_op jit(solution)/shard_map/pallas_call | solution.py:426
  82.6 1.1 %copy.16 = f32[2,4,12,8,512]{4,3,2,1,0:T(8,128)} copy(f32[2,4,12,8,512]{4,3,2,1,0:T(8,128)S(1)} %shard_map.136) | data formatting | bytes 3145728

commit v2 on v1

--- a/solution.py
+++ b/solution.py
@@ -198,12 +198,14 @@
     span = azimuth_dev * blocks
     me = lax.axis_index("space")
     inst_me = lax.axis_index("inst")
-    half = n_space // 2
-    quarter = max(n_space // 4, 1)
-    upper_half = me // half
-    depth = upper_half * (n_space - 1 - me) + (1 - upper_half) * me
+    pairs = n_space // 2
+    pair, side = me // 2, lax.rem(me, 2)
+    quarter = max(pairs // 4, 1)
+    upper_half = pair // max(pairs // 2, 1)
+    depth = upper_half * (pairs - 1 - pair) + (1 - upper_half) * pair
     shift = (depth // quarter) % 2 * (quarter - 1)
     heading = 1 - 2 * upper_half
+    routes = [(step, core) for core in range(2) for step in range(1, pairs)]
     others = range(1, n_space)
 
     def load_state(c):
@@ -229,9 +231,14 @@
     def at(index):
         return pl.ds(pl.multiple_of(index * span, SUBLANE), span)
 
-    def exchange(source, target, send, recv, c, k):
-        step = 1 + lax.rem(k - 1 + shift, n_space - 1)
-        peer = lax.rem(me + heading * step + n_space, n_space)
+    def exchange(source, target, send, recv, c, route):
+        step, core = route
+        if step:
+            step = 1 + lax.rem(step - 1 + shift, pairs - 1)
+            peer = 2 * lax.rem(pair + heading * step + pairs, pairs) + core
+        else:
+            peer = 2 * pair + 1 - side
+        k = 2 * route[0] + core
         return pltpu.make_async_remote_copy(
             src_ref=source.at[c, at(peer)],
             dst_ref=target.at[c, at(me)],
@@ -254,10 +261,17 @@
             device_id={"inst": lax.rem(inst_me + k, n_inst)},
         )
 
+    def send_side(source, target, send, recv, stage, c, core):
+        for route in routes:
+            if route[1] == core:
+                exchange(source, target, send, recv, c, route).start()
+        if core == 0:
+            exchange(source, target, send, recv, c, (0, 0)).start()
+            own(source, target, stage, c).start()
+
     def send_all(source, target, send, recv, stage, c):
-        for k in others:
-            exchange(source, target, send, recv, c, k).start()
-        own(source, target, stage, c).start()
+        for core in range(2):
+            send_side(source, target, send, recv, stage, c, core)
 
     def await_all(source, target, send, recv, stage, c):
         for k in others:
@@ -285,7 +299,9 @@
         pack(c)
         if c == 0:
             pl.semaphore_wait(barrier, n_space - 1 + n_inst - 1)
-        send_all(outgoing, fields, send1, recv1, 0, c)
+        send_side(outgoing, fields, send1, recv1, 0, c, 0)
+    for c in range(chunks):
+        send_side(outgoing, fields, send1, recv1, 0, c, 1)
     for k in range(1, n_inst):
         mate(k).start()
 
@@ -384,9 +400,9 @@
                     + returned[c, pl.ds(row, planes, stride=span), :]
                 )
     for c in range(chunks):
-        for k in others:
-            exchange(outgoing, fields, send1, recv1, c, k).wait_send()
-            exchange(turned, returned, send2, recv2, c, k).wait_send()
+        for route in [(0, 0)] + routes:
+            exchange(outgoing, fields, send1, recv1, c, route).wait_send()
+            exchange(turned, returned, send2, recv2, c, route).wait_send()
 
 
 def on_device(
@@ -484,6 +500,7 @@
     blocks = radial // LANE
     slabs = (
         inst_dev * planes == lax.axis_size("space")
+        and lax.axis_size("space") % 4 == 0
         and lax.axis_size("inst") > 1
         and planes == SUBLANE
         and radial == blocks * LANE

time: 83.9 us -> 80.9 us (0.964)
  Pallas kernels: 81.3 us -> 77.9 us
    pallas_call x1, Pallas kernels: 81.3 us -> 77.9 us  [on_device(): pl.pallas_call(functools.partial(slab_kernel, n_space, n_inst, time_row),...]
where the time goes in v2:
time: 80.9 us; the launch traced here: 80.4 us
  Pallas kernels  77.9 us (96%)
  between operations  1.3 us (2%)
  local copies, waits for them, and re-layouts  1.15 us (1%)
    pallas_call x1, Pallas kernels, on_device(): pl.pallas_call(functools.partial(slab_kernel, n_space, n_inst, time_row),...  77.9 us

profile of v2, /device:TPU:0, one launch (start us, length us, event | category | flops | bytes accessed | tf_op | source)
XLA Modules:
  0.0 80.4 jit_solution(10174957133439033200)
XLA Ops:
  1.3 77.9 %shard_map.136 = f32[2,4,12,8,512]{4,3,2,1,0:T(8,128)S(1)} custom-call(f32[2,4,12,8,512]{4,3,2,1,0:T(8,128)} %state_in.1, f32[512,512]{1,0:T(8,128)} %first_in.1, f32[512,512]{1,0:T(8,128)} %second_in.1, f32[192,512]{1,0:T(8,128)} %bitcast.2, f32[12,512]{1,0:T(8,128)} %radial_flow.1, f32[1,512]{1,0:T(1,128)} %bitcast.3, ...), custom_call_target="tpu_custom_call" | custom-call | tf_op jit(solution)/shard_map/pallas_call | solution.py:442
  79.3 1.1 %copy.16 = f32[2,4,12,8,512]{4,3,2,1,0:T(8,128)} copy(f32[2,4,12,8,512]{4,3,2,1,0:T(8,128)S(1)} %shard_map.136) | data formatting | bytes 3145728
